TPU v7x, 256 devices: a whole 4x4x8 slice. The times are simulated.
256 devices in a mesh: expert: 64 (over y, z, core), tensor: 4 (over x).
Axes of the slice: x: 4, y: 4, z: 8, core: 2. Of those that a mesh axis runs over, the one named last changes fastest.
Arguments:
- attn_heads: bfloat16 [8192, 4096], P('expert', 'tensor'), may hold values from -6 to 6
- out_proj: bfloat16 [4096, 4096], P('tensor', 'expert'), may hold values from -0.09375 to 0.09375
- residual: bfloat16 [8192, 4096], P('expert'), may hold values from -6 to 6
- norm_gain: float32 [4096], replicated, may hold values from 0.1 to 1.9
- route_ids: int32 [8192, 8], P('expert'), may hold values from 0 to 63, all different within a row; in each aligned block of 128 rows (0 to 127, 128 to 255, ...) at most 18 rows name the same one
- route_weights: float32 [8192, 8], P('expert'), may hold values from 0.05 to 1
- w_gate: bfloat16 [64, 4096, 1536], P('expert', None, 'tensor'), may hold values from -0.09375 to 0.09375
- w_up: bfloat16 [64, 4096, 1536], P('expert', None, 'tensor'), may hold values from -0.09375 to 0.09375
- w_down: bfloat16 [64, 1536, 4096], P('expert', 'tensor'), may hold values from -0.15625 to 0.15625
Outputs:
- layer_out: bfloat16 [8192, 4096], P('expert', 'tensor')
Inputs may be any that keep to these rules, and one draw needn't show every extreme that they name: `route_ids`: each row names 8 different experts. In aligned blocks of 128 rows no expert is named more than 18 times, a bound that some block reaches.
All inputs are finite; a program needn't handle non-finite values.
Results may differ from a plain program's by a relative error of at most 0.015.
Values may be sent and summed in bfloat16 or wider, within the bound.
A program may use at most 128 MiB of HBM per device.

v0:
```python
import jax
import jax.numpy as jnp
from jax import lax
from jax.sharding import PartitionSpec as P

EXPERTS = 64
MAIN = 16
OVER = 2
LANES = 128


def routing(route_ids, route_weights):
    count = route_ids.shape[0]
    hits = (route_ids[:, :, None] == jnp.arange(EXPERTS, dtype=jnp.int32)[None, None, :]).astype(
        jnp.float32
    )
    chosen = jnp.sum(hits, axis=1)
    weights = route_weights / jnp.sum(route_weights, axis=-1, keepdims=True)
    weight = jnp.sum(hits * weights[:, :, None], axis=1)
    order = jnp.arange(count, dtype=jnp.int32)
    earlier = (order[None, :] < order[:, None]).astype(jnp.bfloat16)
    rank = jnp.dot(earlier, chosen.astype(jnp.bfloat16), preferred_element_type=jnp.float32)
    rank = jnp.where(chosen > 0, rank, -1.0)
    return (rank.astype(jnp.int32), weight)


def per_device(
    attn_heads, out_proj, residual, norm_gain, route_ids, route_weights, w_gate, w_up, w_down
):
    tokens, model_width = residual.shape
    members = lax.axis_size("tensor")
    member = lax.axis_index("tensor")
    cols = model_width // members
    groups = cols // LANES
    rows = EXPERTS * MAIN
    rank, weight = routing(route_ids, route_weights)
    row = jnp.arange(rows, dtype=jnp.int32)
    slot = row % MAIN
    spread = jnp.repeat(rank, MAIN, axis=1)
    main_hit = spread == slot[None, :]
    over_hit = spread == (MAIN + slot // groups)[None, :]
    row_weight = jnp.repeat(weight, MAIN, axis=1)
    heads_out = jnp.dot(
        attn_heads,
        lax.all_gather(out_proj, "expert", axis=1, tiled=True),
        preferred_element_type=jnp.float32,
    ).astype(jnp.bfloat16)
    attn_out = lax.psum_scatter(
        jnp.transpose(heads_out.reshape(tokens, members, cols), (1, 0, 2)),
        "tensor",
        scatter_dimension=0,
        tiled=True,
    )[0].astype(jnp.float32)
    own_residual = lax.dynamic_slice_in_dim(residual, member * cols, cols, 1)
    own_gain = lax.dynamic_slice_in_dim(norm_gain, member * cols, cols, 0)
    hidden = own_residual.astype(jnp.float32) + attn_out
    squares = lax.psum(jnp.sum(hidden * hidden, axis=-1, keepdims=True), "tensor")
    normed = (hidden * lax.rsqrt(squares / model_width + 1e-06) * own_gain).astype(jnp.bfloat16)
    main = jnp.einsum(
        "tr,td->rd", main_hit.astype(jnp.bfloat16), normed, preferred_element_type=jnp.float32
    ).astype(jnp.bfloat16)
    wide = jnp.einsum(
        "tr,td->rd", over_hit.astype(jnp.bfloat16), normed, preferred_element_type=jnp.float32
    ).astype(jnp.bfloat16)
    own_group = (row % groups)[:, None]
    over = jnp.zeros((rows, LANES), jnp.bfloat16)
    for g in range(groups):
        over = jnp.where(own_group == g, wide[:, g * LANES : (g + 1) * LANES], over)
    packed = jnp.concatenate([main, over], axis=1).reshape(EXPERTS, MAIN, cols + LANES)
    arrived = lax.all_to_all(packed, "expert", split_axis=0, concat_axis=0, tiled=True)
    full = lax.all_gather(arrived.reshape(rows, cols + LANES), "tensor", axis=0)
    main_in = jnp.concatenate([full[m, :, :cols] for m in range(members)], axis=1)
    over_in = jnp.transpose(
        full[:, :, cols:].reshape(members, EXPERTS * OVER, groups, LANES), (1, 0, 2, 3)
    ).reshape(EXPERTS * OVER, model_width)
    inputs = jnp.concatenate([main_in, over_in], axis=0)
    gate = jnp.dot(inputs, w_gate[0], preferred_element_type=jnp.float32)
    up = jnp.dot(inputs, w_up[0], preferred_element_type=jnp.float32)
    act = (jax.nn.silu(gate) * up).astype(jnp.bfloat16)
    down = w_down[0].reshape(-1, members, cols)
    parts = jnp.stack(
        [jnp.dot(act, down[:, m], preferred_element_type=jnp.float32) for m in range(members)]
    ).astype(jnp.bfloat16)
    summed = lax.psum_scatter(parts, "tensor", scatter_dimension=0, tiled=True)[0]
    back = jnp.concatenate([summed[:rows], summed[rows:].reshape(rows, LANES)], axis=1).reshape(
        EXPERTS, MAIN, cols + LANES
    )
    returned = lax.all_to_all(back, "expert", split_axis=0, concat_axis=0, tiled=True).reshape(
        rows, cols + LANES
    )
    high = row_weight.astype(jnp.bfloat16)
    low = (row_weight - high.astype(jnp.float32)).astype(jnp.bfloat16)
    mixture = 0.0
    zero = jnp.zeros((), jnp.bfloat16)
    for part in (high, low):
        pick = jnp.where(main_hit, part, zero)
        mixture += jnp.dot(pick, returned[:, :cols], preferred_element_type=jnp.float32)
        extra = [
            jnp.dot(
                jnp.where(over_hit & (row % groups == g)[None, :], part, zero),
                returned[:, cols:],
                preferred_element_type=jnp.float32,
            )
            for g in range(groups)
        ]
        mixture += jnp.concatenate(extra, axis=1)
    return (hidden + mixture).astype(jnp.bfloat16)


def solution(mesh):
    placed = (
        P("expert", "tensor"),
        P("tensor", "expert"),
        P("expert", None),
        P(),
        P("expert", None),
        P("expert", None),
        P("expert", None, "tensor"),
        P("expert", None, "tensor"),
        P("expert", "tensor", None),
    )
    return jax.shard_map(
        per_device, mesh=mesh, in_specs=placed, out_specs=P("expert", "tensor"), check_vma=False
    )
```

profile of v0, /device:TPU:1, one launch (start us, length us, event | category | flops | bytes accessed | tf_op | source)
XLA Modules:
  0.0 545.0 jit_solution(5907444600638670567)
XLA Ops:
  6.5 0.7 all-gather.3.cloned.1.call-update
  7.3 0.0 reduce-scatter.3.cloned.1.call-start
  7.3 90.1 %all-gather.3.cloned.1.call-done = bf16[1024,4096]{0,1:T(8,128)(2,1)} async-done(((bf16[1024,64]{0,1:T(8,128)(2,1)}), bf16[1024,4096]{0,1:T(8,128)(2,1)}) %all-gather.3.cloned.1.call-update) | async-done | bytes 8388624 | tf_op jit(solution)/shard_map/all_gather | solution.py:45
  97.5 6.3 %convolution_convert_fusion = bf16[128,4096]{1,0:T(8,128)(2,1)S(1)} fusion(bf16[128,1024]{1,0:T(8,128)(2,1)} %param.9, bf16[1024,4096]{0,1:T(8,128)(2,1)} %all-gather.3.cloned.1.call-done), kind=kOutput, calls=%fused_computation.2 | convolution fusion | flops 1074266112 | bytes 9699328 | tf_op jit(solution)/shard_map/dot_general | solution.py:43
  103.8 1.1 copy.173
  104.9 0.0 all-gather.5.cloned.1.call-start
  105.0 0.7 dynamic_slice.7
  105.7 0.7 convert_reduce_fusion
  106.4 0.1 fusion.29
  106.5 0.6 copy-done.21
  107.1 1.3 bitcast_compare_fusion.1
  108.4 0.6 fusion.76
  109.0 0.6 fusion.74
  109.6 0.6 fusion.72
  110.2 0.6 fusion.70
  110.8 15.7 %reduce-scatter.3.cloned.1.call-done = bf16[1,128,1024]{2,1,0:T(8,128)(2,1)} async-done(((bf16[4,128,1024]{2,1,0:T(8,128)(2,1)}), bf16[1,128,1024]{2,1,0:T(8,128)(2,1)}) %reduce-scatter.3.cloned.1.call-update) | async-done | bytes 262160 | tf_op jit(solution)/shard_map/reduce_scatter | solution.py:48
  126.5 1.2 multiply_reduce_fusion
  127.7 6.5 %psum.7 = f32[128,1]{0,1:T(1,128)S(1)} all-reduce(f32[128,1]{0,1:T(1,128)S(1)} %bitcast.221), channel_id=1, replica_groups=mesh['expert'=64,'tensor'=4] {'tensor'}, use_global_device_ids=true, to_apply=%region_5.6 | all-reduce | flops 128 | bytes 1024 | tf_op jit(solution)/shard_map/psum | solution.py:57
  134.3 2.0 convolution_convert_fusion.5
  136.3 0.2 fusion.64
  136.6 1.8 convolution_convert_fusion.6
  138.3 1.7 pad_maximum_fusion.2
  140.0 4.4 copy.131
  144.3 71.2 %all_to_all.10 = bf16[64,16,1152]{2,1,0:T(8,128)(2,1)} all-to-all(bf16[64,16,1152]{2,1,0:T(8,128)(2,1)} %bitcast.212), channel_id=1, replica_groups=mesh['expert'=64,'tensor'=4] {'expert'}, dimensions={0} | all-to-all | bytes 4718592 | tf_op jit(solution)/shard_map/all_to_all | solution.py:70
  215.5 0.2 reduce-scatter.5.cloned.1.call-start
  215.8 4.7 copy.134
  220.5 84.6 %all-gather.5.cloned.1.call-done = bf16[4,1024,1152]{2,1,0:T(8,128)(2,1)} async-done(((bf16[1,1024,1152]{2,1,0:T(8,128)(2,1)}), bf16[4,1024,1152]{2,1,0:T(8,128)(2,1)}) %all-gather.5.cloned.1.call-update) | async-done | bytes 9437200 | tf_op jit(solution)/shard_map/all_gather | solution.py:71
  305.1 2.3 slice_bitcast_fusion.4
  307.3 2.4 copy.132
  309.8 2.3 copy.133
  312.1 4.9 slice_bitcast_fusion.3
  317.0 19.2 %fusion.5 = f32[1152,384]{1,0:T(8,128)} fusion(bf16[1,4096,384]{2,1,0:T(8,128)(2,1)S(1)} %copy-done, bf16[128,4096]{1,0:T(8,128)(2,1)S(1)} %copy-done.19, bf16[1024,1024]{1,0:T(8,128)(2,1)S(1)} %get-tuple-element.8, bf16[1024,1024]{1,0:T(8,128)(2,1)S(1)} %get-tuple-element.9, bf16[1024,1024]{1,0:T(8,128)(2,1)} %get-tuple-element.10, ...), kind=kOutput, calls=%fused_computation.13 | convolution fusion | flops 3671064576 | bytes 14352384 | tf_op jit(solution)/shard_map/dot_general | solution.py:77
  336.3 16.9 %fusion.7 = bf16[1152,384]{1,0:T(8,128)(2,1)} fusion(bf16[1,4096,384]{2,1,0:T(8,128)(2,1)} %param.16, f32[1152,384]{1,0:T(8,128)} %fusion.5, bf16[128,4096]{1,0:T(8,128)(2,1)S(1)} %copy-done.19, bf16[1024,1024]{1,0:T(8,128)(2,1)S(1)} %get-tuple-element.8, bf16[1024,1024]{1,0:T(8,128)(2,1)S(1)} %get-tuple-element.9, ...), kind=kOutput, calls=%fused_computation.15 | convolution fusion | flops 3673718784 | bytes 15237120 | tf_op jit(solution)/shard_map/dot_general | solution.py:78
  353.2 2.7 fusion.3
  355.8 1.4 fusion.2
  357.3 1.4 fusion.1
  358.7 1.4 fusion
  360.1 4.6 pad_maximum_fusion.1
  364.7 92.7 %reduce-scatter.5.cloned.1.call-done = bf16[1,1152,1024]{2,1,0:T(8,128)(2,1)} async-done(((bf16[4,1152,1024]{2,1,0:T(8,128)(2,1)}), bf16[1,1152,1024]{2,1,0:T(8,128)(2,1)}) %reduce-scatter.5.cloned.1.call-update) | async-done | bytes 2359312 | tf_op jit(solution)/shard_map/reduce_scatter | solution.py:84
  457.4 1.0 slice.120
  458.4 0.1 concatenate.27
  458.5 1.5 slice-done
  460.0 1.7 pad_maximum_fusion.3
  461.7 10.6 %all-to-all-start.1 = ((bf16[64,16,1152]{2,1,0:T(8,128)(2,1)}), bf16[64,16,1152]{2,1,0:T(8,128)(2,1)S(1)}, u32[]{:S(2)}, u32[]{:S(2)}) async-start(bf16[64,16,1152]{2,1,0:T(8,128)(2,1)} %pad_maximum_fusion.3), calls=%async_computation.3 | async-start | bytes 4718592 | tf_op jit(solution)/shard_map/all_to_all | solution.py:88
  472.5 4.6 fusion.39
  477.1 51.9 %all-to-all-done.1 = bf16[64,16,1152]{2,1,0:T(8,128)(2,1)S(1)} async-done(((bf16[64,16,1152]{2,1,0:T(8,128)(2,1)}), bf16[64,16,1152]{2,1,0:T(8,128)(2,1)S(1)}, u32[]{:S(2)}, u32[]{:S(2)}) %all-to-all-start.1) | async-done | bytes 2359328 | tf_op jit(solution)/shard_map/all_to_all | solution.py:88
  529.1 1.7 fusion.10
  530.9 0.3 convolution_dynamic-update-slice_fusion.15
  531.2 0.3 convolution_dynamic-update-slice_fusion.7
  531.5 0.3 convolution_dynamic-update-slice_fusion.14
  531.8 0.3 convolution_dynamic-update-slice_fusion.13
  532.1 0.3 convolution_dynamic-update-slice_fusion.12
  532.3 0.3 convolution_dynamic-update-slice_fusion.11
  532.6 0.3 convolution_dynamic-update-slice_fusion.10
  532.9 0.3 convolution_dynamic-update-slice_fusion.9
  533.2 0.3 convolution_dynamic-update-slice_fusion.8
  533.5 0.3 convolution_dynamic-update-slice_fusion.6
  533.8 0.3 convolution_dynamic-update-slice_fusion.5
  534.1 0.3 convolution_dynamic-update-slice_fusion.4
  534.3 0.3 convolution_dynamic-update-slice_fusion.3
  534.6 0.3 convolution_dynamic-update-slice_fusion.2
  534.9 0.3 convolution_dynamic-update-slice_fusion.1
  535.2 0.3 convolution_dynamic-update-slice_fusion
  535.5 3.0 fusion.26
  (88 shorter events, 0.3 us)
Async XLA Ops:
  6.5 310.5 %copy-start = (bf16[1,4096,384]{2,1,0:T(8,128)(2,1)S(1)}, bf16[1,4096,384]{2,1,0:T(8,128)(2,1)}, u32[]{:S(2)}) copy-start(bf16[1,4096,384]{2,1,0:T(8,128)(2,1)} %param.15) | copy-start | bytes 9437188
  6.5 90.9 %all-gather.3.cloned.1.call-start = ((), (), s32[]{:S(2)}) async-start(), calls=%async_computation.4 | async-start | bytes 8519680 | tf_op jit(solution)/shard_map/all_gather | solution.py:45
  7.3 119.3 %reduce-scatter.3.cloned.1.call-start = ((), (), s32[]{:S(2)}) async-start(), calls=%async_computation.5 | async-start | bytes 1310720 | tf_op jit(solution)/shard_map/reduce_scatter | solution.py:48
  103.8 1.2 copy-start.23
  103.8 1.9 copy-start.38
  104.9 200.2 %all-gather.5.cloned.1.call-start = ((), (), s32[]{:S(2)}) async-start(), calls=%async_computation.6 | async-start | bytes 11796480 | tf_op jit(solution)/shard_map/all_gather | solution.py:71
  106.5 0.6 copy-start.21
  134.2 2.0 copy-start.24
  134.2 2.0 copy-start.26
  134.2 2.1 copy-start.28
  134.2 2.1 copy-start.30
  134.2 2.1 copy-start.32
  134.3 2.1 copy-start.34
  134.3 2.1 copy-start.36
  134.3 2.3 copy-start.3
  215.5 241.9 %reduce-scatter.5.cloned.1.call-start = ((), (), s32[]{:S(2)}) async-start(), calls=%async_computation.7 | async-start | bytes 11796480 | tf_op jit(solution)/shard_map/reduce_scatter | solution.py:84
  312.1 5.0 copy-start.19
  336.3 16.9 %copy-start.4 = (bf16[1,384,4096]{1,2,0:T(8,128)(2,1)S(1)}, bf16[1,384,4096]{1,2,0:T(8,128)(2,1)}, u32[]{:S(2)}) copy-start(bf16[1,384,4096]{1,2,0:T(8,128)(2,1)} %copy.134) | copy-start | bytes 9437188
  353.1 2.7 copy-start.39
  458.4 1.6 slice-start
  461.7 10.7 %copy-start.20 = (f32[128,64]{0,1:T(8,128)S(1)}, f32[128,64]{0,1:T(8,128)}, u32[]{:S(2)}) copy-start(f32[128,64]{0,1:T(8,128)} %get-tuple-element.6) | copy-start | bytes 98308
  461.7 10.7 %copy-start.22 = (s32[128,64]{0,1:T(8,128)S(1)}, s32[128,64]{0,1:T(8,128)}, u32[]{:S(2)}) copy-start(s32[128,64]{0,1:T(8,128)} %copy-done.21) | copy-start | bytes 98308
  461.7 10.7 %copy-start.25 = (pred[1024]{0:T(1024)(128)(4,1)S(1)}, pred[1024]{0:T(1024)(128)(4,1)}, u32[]{:S(2)}) copy-start(pred[1024]{0:T(1024)(128)(4,1)} %get-tuple-element.70) | copy-start | bytes 3076
  461.7 10.7 %copy-start.27 = (pred[1024]{0:T(1024)(128)(4,1)S(1)}, pred[1024]{0:T(1024)(128)(4,1)}, u32[]{:S(2)}) copy-start(pred[1024]{0:T(1024)(128)(4,1)} %get-tuple-element.67) | copy-start | bytes 3076
  461.7 10.7 %copy-start.29 = (pred[1024]{0:T(1024)(128)(4,1)S(1)}, pred[1024]{0:T(1024)(128)(4,1)}, u32[]{:S(2)}) copy-start(pred[1024]{0:T(1024)(128)(4,1)} %get-tuple-element.68) | copy-start | bytes 3076
  461.7 10.7 %copy-start.31 = (pred[1024]{0:T(1024)(128)(4,1)S(1)}, pred[1024]{0:T(1024)(128)(4,1)}, u32[]{:S(2)}) copy-start(pred[1024]{0:T(1024)(128)(4,1)} %get-tuple-element.65) | copy-start | bytes 3076
  461.7 10.7 %copy-start.33 = (pred[1024]{0:T(1024)(128)(4,1)S(1)}, pred[1024]{0:T(1024)(128)(4,1)}, u32[]{:S(2)}) copy-start(pred[1024]{0:T(1024)(128)(4,1)} %get-tuple-element.66) | copy-start | bytes 3076
  461.7 10.7 %copy-start.35 = (pred[1024]{0:T(1024)(128)(4,1)S(1)}, pred[1024]{0:T(1024)(128)(4,1)}, u32[]{:S(2)}) copy-start(pred[1024]{0:T(1024)(128)(4,1)} %get-tuple-element.63) | copy-start | bytes 3076
  461.7 10.7 %copy-start.37 = (pred[1024]{0:T(1024)(128)(4,1)S(1)}, pred[1024]{0:T(1024)(128)(4,1)}, u32[]{:S(2)}) copy-start(pred[1024]{0:T(1024)(128)(4,1)} %get-tuple-element.64) | copy-start | bytes 3076
  461.7 67.3 %all-to-all-start.1 = ((bf16[64,16,1152]{2,1,0:T(8,128)(2,1)}), bf16[64,16,1152]{2,1,0:T(8,128)(2,1)S(1)}, u32[]{:S(2)}, u32[]{:S(2)}) async-start(bf16[64,16,1152]{2,1,0:T(8,128)(2,1)} %pad_maximum_fusion.3), calls=%async_computation.3 | async-start | bytes 4718592 | tf_op jit(solution)/shard_map/all_to_all | solution.py:88
  529.0 6.1 %copy-start.2 = (bf16[64,16,1152]{2,1,0:T(8,128)(2,1)}, bf16[64,16,1152]{2,1,0:T(8,128)(2,1)S(1)}, u32[]{:S(2)}) copy-start(bf16[64,16,1152]{2,1,0:T(8,128)(2,1)S(1)} %all-to-all-done.1) | copy-start | bytes 7077892
  529.0 1.8 copy-start.18
  529.0 2.1 copy-start.17
  529.0 2.4 copy-start.16
  529.1 2.7 copy-start.15
  529.1 3.0 copy-start.14
  529.1 3.3 copy-start.13
  530.8 1.8 copy-start.12
  530.9 2.0 copy-start.11
  530.9 2.3 copy-start.10
  531.2 2.3 copy-start.9
  531.5 2.3 copy-start.8
  531.7 2.3 copy-start.7
  532.0 2.3 copy-start.6
  533.2 2.3 copy-start.5
  535.5 3.0 copy-start.1
Sparse Core Ops, SparseCore 0:
  10.1 87.2 all-gather.2
  105.0 21.4 reduce-scatter.2
  215.7 89.3 all-gather.4
  364.8 92.5 reduce-scatter.4
where the time goes:
time: 546 us; the launch traced here: 545 us
  waiting for transfers between devices  336 us (62%)
  blocking collectives  77.7 us (14%)
  matrix products  62.3 us (11%)
  local copies, waits for them, and re-layouts  26.1 us (5%)
  other arithmetic  18.2 us (3%)
  between operations  13.9 us (3%)
  starting transfers between devices  11 us (2%)
    reduce_scatter x1, waiting for transfers between devices, per_device(): lax.psum_scatter(parts, 'tensor', scatter_dimension=0, tiled=True)[0]  92.7 us
    all_gather x1, waiting for transfers between devices, per_device(): lax.all_gather(out_proj, 'expert', axis=1, tiled=True)  90.1 us
    all_gather x1, waiting for transfers between devices, per_device(): full = lax.all_gather(arrived.reshape(rows, cols + LANES), 'tensor', axis=0)  84.6 us
    all_to_all x1, blocking collectives, per_device(): lax.all_to_all(packed, 'expert', split_axis=0, concat_axis=0, tiled=True)  71.2 us
    all_to_all x1, waiting for transfers between devices, per_device(): lax.all_to_all(back, 'expert', split_axis=0, concat_axis=0, tiled=True)  51.9 us
    dot_general x1, matrix products, per_device(): gate = jnp.dot(inputs, w_gate[0], preferred_element_type=jnp.float32)  19.2 us
    dot_general x1, matrix products, per_device(): up = jnp.dot(inputs, w_up[0], preferred_element_type=jnp.float32)  16.9 us
    reduce_scatter x1, waiting for transfers between devices, per_device(): lax.psum_scatter(jnp.transpose(heads_out.reshape(tokens, members, cols),...  15.7 us
  transfers between devices with their start and end apart: 5, of which 5 were waited for; matrix products, arithmetic and copies ran while one was open for 3% of the time, Pallas kernels for 0%

commit v1 on v0

--- a/solution.py
+++ b/solution.py
@@ -42,7 +42,9 @@
     row_weight = jnp.repeat(weight, MAIN, axis=1)
     heads_out = jnp.dot(
         attn_heads,
-        lax.all_gather(out_proj, "expert", axis=1, tiled=True),
+        jnp.concatenate(
+            lax.all_to_all(jnp.stack([out_proj] * lax.axis_size("expert")), "expert", 0, 0), axis=1
+        ),
         preferred_element_type=jnp.float32,
     ).astype(jnp.bfloat16)
     attn_out = lax.psum_scatter(

time: 546 us -> 653 us (1.20)
  blocking collectives: 77.7 us -> 277 us
  waiting for transfers between devices: 336 us -> 245 us
    all_to_all x0 -> x1, blocking collectives: none -> 199 us  [per_device(): lax.all_to_all(jnp.stack([out_proj] * lax.axis_size('expert')), 'expert',...]
    all_gather x1 -> x0, waiting for transfers between devices: 90.1 us -> none  [per_device(): lax.all_gather(out_proj, 'expert', axis=1, tiled=True)]
  transfers between devices with their start and end apart: 5 -> 4, of which waited for: 5 -> 4; matrix products, arithmetic and copies ran while one was open for 3% -> 2% of each run, Pallas kernels for 0% -> 0%
where the time goes in v1:
time: 653 us; the launch traced here: 652 us
  blocking collectives  277 us (42%)
  waiting for transfers between devices  245 us (38%)
  matrix products  59.7 us (9%)
  local copies, waits for them, and re-layouts  28.2 us (4%)
  other arithmetic  18.1 us (3%)
  between operations  13.8 us (2%)
  starting transfers between devices  10.9 us (2%)
    all_to_all x1, blocking collectives, per_device(): lax.all_to_all(jnp.stack([out_proj] * lax.axis_size('expert')), 'expert',...  199 us
    reduce_scatter x1, waiting for transfers between devices, per_device(): lax.psum_scatter(parts, 'tensor', scatter_dimension=0, tiled=True)[0]  92.7 us
    all_gather x1, waiting for transfers between devices, per_device(): full = lax.all_gather(arrived.reshape(rows, cols + LANES), 'tensor', axis=0)  84.6 us
    all_to_all x1, blocking collectives, per_device(): lax.all_to_all(packed, 'expert', split_axis=0, concat_axis=0, tiled=True)  71 us
    all_to_all x1, waiting for transfers between devices, per_device(): lax.all_to_all(back, 'expert', split_axis=0, concat_axis=0, tiled=True)  52 us
    dot_general x1, matrix products, per_device(): gate = jnp.dot(inputs, w_gate[0], preferred_element_type=jnp.float32)  19.2 us
    dot_general x1, matrix products, per_device(): up = jnp.dot(inputs, w_up[0], preferred_element_type=jnp.float32)  16.9 us
    reduce_scatter x1, waiting for transfers between devices, per_device(): lax.psum_scatter(jnp.transpose(heads_out.reshape(tokens, members, cols),...  15.4 us
  transfers between devices with their start and end apart: 4, of which 4 were waited for; matrix products, arithmetic and copies ran while one was open for 2% of the time, Pallas kernels for 0%

profile of v1, /device:TPU:1, one launch (start us, length us, event | category | flops | bytes accessed | tf_op | source)
XLA Modules:
  0.0 652.4 jit_solution(4091422079002573747)
XLA Ops:
  6.5 2.1 stack.17
  8.7 199.2 %all_to_all.15 = bf16[64,1024,64]{1,2,0:T(8,128)(2,1)S(1)} all-to-all(bf16[64,1024,64]{1,2,0:T(8,128)(2,1)S(1)} %stack.17), channel_id=1, replica_groups=mesh['expert'=64,'tensor'=4] {'expert'}, dimensions={0} | all-to-all | bytes 16777216 | tf_op jit(solution)/shard_map/all_to_all | solution.py:46
  207.8 2.8 convolution_convert_fusion
  210.7 1.1 copy.174
  211.8 0.0 all-gather.2.cloned.1.call-start
  211.9 0.7 dynamic_slice.7
  212.6 0.7 convert_reduce_fusion
  213.3 0.1 fusion.29
  213.4 0.6 copy-done.20
  214.0 1.3 bitcast_compare_fusion.1
  215.3 0.6 fusion.70
  215.9 0.6 fusion.72
  216.5 0.6 fusion.74
  217.1 0.6 fusion.76
  217.7 15.4 %reduce-scatter.3.cloned.1.call-done = bf16[1,128,1024]{2,1,0:T(8,128)(2,1)} async-done(((bf16[4,128,1024]{2,1,0:T(8,128)(2,1)}), bf16[1,128,1024]{2,1,0:T(8,128)(2,1)}) %reduce-scatter.3.cloned.1.call-update) | async-done | bytes 262160 | tf_op jit(solution)/shard_map/reduce_scatter | solution.py:50
  233.1 1.2 multiply_reduce_fusion
  234.3 6.7 %psum.7 = f32[128,1]{0,1:T(1,128)S(1)} all-reduce(f32[128,1]{0,1:T(1,128)S(1)} %bitcast.225), channel_id=1, replica_groups=mesh['expert'=64,'tensor'=4] {'tensor'}, use_global_device_ids=true, to_apply=%region_5.6 | all-reduce | flops 128 | bytes 1024 | tf_op jit(solution)/shard_map/psum | solution.py:59
  241.0 2.0 convolution_convert_fusion.5
  243.0 0.2 fusion.64
  243.3 1.8 convolution_convert_fusion.6
  245.1 1.6 pad_maximum_fusion.2
  246.7 4.3 copy.132
  251.0 71.0 %all_to_all.16 = bf16[64,16,1152]{2,1,0:T(8,128)(2,1)} all-to-all(bf16[64,16,1152]{2,1,0:T(8,128)(2,1)} %bitcast.216), channel_id=1, replica_groups=mesh['expert'=64,'tensor'=4] {'expert'}, dimensions={0} | all-to-all | bytes 4718592 | tf_op jit(solution)/shard_map/all_to_all | solution.py:72
  322.0 0.0 all-gather.2.cloned.1.call-update
  322.0 0.2 reduce-scatter.5.cloned.1.call-start
  322.3 4.7 copy.135
  326.9 84.6 %all-gather.2.cloned.1.call-done = bf16[4,1024,1152]{2,1,0:T(8,128)(2,1)} async-done(((bf16[1,1024,1152]{2,1,0:T(8,128)(2,1)}), bf16[4,1024,1152]{2,1,0:T(8,128)(2,1)}) %all-gather.2.cloned.1.call-update) | async-done | bytes 9437200 | tf_op jit(solution)/shard_map/all_gather | solution.py:73
  411.6 2.3 slice_bitcast_fusion.4
  413.9 2.4 copy.133
  416.3 2.3 copy.134
  418.5 5.0 slice_bitcast_fusion.3
  423.5 19.2 %fusion.5 = f32[1152,384]{1,0:T(8,128)} fusion(bf16[1,4096,384]{2,1,0:T(8,128)(2,1)S(1)} %copy-done, bf16[128,4096]{1,0:T(8,128)(2,1)S(1)} %copy-done.18, bf16[1024,1024]{1,0:T(8,128)(2,1)S(1)} %get-tuple-element.8, bf16[1024,1024]{1,0:T(8,128)(2,1)S(1)} %get-tuple-element.9, bf16[1024,1024]{1,0:T(8,128)(2,1)} %get-tuple-element.10, ...), kind=kOutput, calls=%fused_computation.13 | convolution fusion | flops 3671064576 | bytes 14352384 | tf_op jit(solution)/shard_map/dot_general | solution.py:79
  442.8 16.9 %fusion.7 = bf16[1152,384]{1,0:T(8,128)(2,1)} fusion(bf16[1,4096,384]{2,1,0:T(8,128)(2,1)} %param.16, f32[1152,384]{1,0:T(8,128)} %fusion.5, bf16[128,4096]{1,0:T(8,128)(2,1)S(1)} %copy-done.18, bf16[1024,1024]{1,0:T(8,128)(2,1)S(1)} %get-tuple-element.8, bf16[1024,1024]{1,0:T(8,128)(2,1)S(1)} %get-tuple-element.9, ...), kind=kOutput, calls=%fused_computation.15 | convolution fusion | flops 3673718784 | bytes 15237120 | tf_op jit(solution)/shard_map/dot_general | solution.py:80
  459.6 2.7 fusion
  462.3 1.4 fusion.1
  463.8 1.4 fusion.2
  465.2 1.4 fusion.3
  466.6 4.5 pad_maximum_fusion.1
  471.2 92.7 %reduce-scatter.5.cloned.1.call-done = bf16[1,1152,1024]{2,1,0:T(8,128)(2,1)} async-done(((bf16[4,1152,1024]{2,1,0:T(8,128)(2,1)}), bf16[1,1152,1024]{2,1,0:T(8,128)(2,1)}) %reduce-scatter.5.cloned.1.call-update) | async-done | bytes 2359312 | tf_op jit(solution)/shard_map/reduce_scatter | solution.py:86
  563.9 1.0 slice.120
  564.9 0.1 concatenate.27
  565.1 1.5 slice-done
  566.5 1.7 pad_maximum_fusion.3
  568.2 10.6 %all-to-all-start.2 = ((bf16[64,16,1152]{2,1,0:T(8,128)(2,1)}), bf16[64,16,1152]{2,1,0:T(8,128)(2,1)S(1)}, u32[]{:S(2)}, u32[]{:S(2)}) async-start(bf16[64,16,1152]{2,1,0:T(8,128)(2,1)} %pad_maximum_fusion.3), calls=%async_computation.4 | async-start | bytes 4718592 | tf_op jit(solution)/shard_map/all_to_all | solution.py:90
  579.0 4.5 fusion.39
  583.5 52.0 %all-to-all-done.2 = bf16[64,16,1152]{2,1,0:T(8,128)(2,1)S(1)} async-done(((bf16[64,16,1152]{2,1,0:T(8,128)(2,1)}), bf16[64,16,1152]{2,1,0:T(8,128)(2,1)S(1)}, u32[]{:S(2)}, u32[]{:S(2)}) %all-to-all-start.2) | async-done | bytes 2359328 | tf_op jit(solution)/shard_map/all_to_all | solution.py:90
  635.6 1.5 convolution_dynamic-update-slice_fusion.15
  637.1 1.5 fusion.10
  638.6 0.3 convolution_dynamic-update-slice_fusion.7
  638.9 0.3 convolution_dynamic-update-slice_fusion.14
  639.2 0.3 convolution_dynamic-update-slice_fusion.13
  639.5 0.3 convolution_dynamic-update-slice_fusion.12
  639.8 0.3 convolution_dynamic-update-slice_fusion.11
  640.0 0.3 convolution_dynamic-update-slice_fusion.10
  640.3 0.3 convolution_dynamic-update-slice_fusion.9
  640.6 0.3 convolution_dynamic-update-slice_fusion.8
  640.9 0.3 convolution_dynamic-update-slice_fusion.6
  641.2 0.3 convolution_dynamic-update-slice_fusion.5
  641.5 0.3 convolution_dynamic-update-slice_fusion.4
  641.8 0.3 convolution_dynamic-update-slice_fusion.3
  642.1 0.3 convolution_dynamic-update-slice_fusion.2
  642.3 0.3 convolution_dynamic-update-slice_fusion.1
  642.6 0.3 convolution_dynamic-update-slice_fusion
  642.9 3.0 fusion.26
  (87 shorter events, 0.2 us)
Async XLA Ops:
  6.5 417.0 %copy-start = (bf16[1,4096,384]{2,1,0:T(8,128)(2,1)S(1)}, bf16[1,4096,384]{2,1,0:T(8,128)(2,1)}, u32[]{:S(2)}) copy-start(bf16[1,4096,384]{2,1,0:T(8,128)(2,1)} %param.15) | copy-start | bytes 9437188
  6.5 226.6 %reduce-scatter.3.cloned.1.call-start = ((), (), s32[]{:S(2)}) async-start(), calls=%async_computation.5 | async-start | bytes 1310720 | tf_op jit(solution)/shard_map/reduce_scatter | solution.py:50
  8.7 199.2 %copy-start.22 = (bf16[128,1024]{1,0:T(8,128)(2,1)S(1)}, bf16[128,1024]{1,0:T(8,128)(2,1)}, u32[]{:S(2)}) copy-start(bf16[128,1024]{1,0:T(8,128)(2,1)} %param.9) | copy-start | bytes 786436
  210.7 1.9 copy-start.23
  210.7 1.9 copy-start.38
  211.8 199.7 %all-gather.2.cloned.1.call-start = ((), (), s32[]{:S(2)}) async-start(), calls=%async_computation.6 | async-start | bytes 11796480 | tf_op jit(solution)/shard_map/all_gather | solution.py:73
  213.4 0.6 copy-start.20
  240.9 2.0 copy-start.24
  240.9 2.0 copy-start.26
  240.9 2.1 copy-start.28
  240.9 2.1 copy-start.30
  241.0 2.1 copy-start.32
  241.0 2.1 copy-start.34
  241.0 2.1 copy-start.36
  241.0 2.3 copy-start.3
  322.0 241.9 %reduce-scatter.5.cloned.1.call-start = ((), (), s32[]{:S(2)}) async-start(), calls=%async_computation.7 | async-start | bytes 11796480 | tf_op jit(solution)/shard_map/reduce_scatter | solution.py:86
  418.5 5.0 copy-start.18
  442.8 16.9 %copy-start.4 = (bf16[1,384,4096]{1,2,0:T(8,128)(2,1)S(1)}, bf16[1,384,4096]{1,2,0:T(8,128)(2,1)}, u32[]{:S(2)}) copy-start(bf16[1,384,4096]{1,2,0:T(8,128)(2,1)} %copy.135) | copy-start | bytes 9437188
  459.6 2.7 copy-start.39
  564.9 1.6 slice-start
  568.2 10.7 %copy-start.19 = (f32[128,64]{0,1:T(8,128)S(1)}, f32[128,64]{0,1:T(8,128)}, u32[]{:S(2)}) copy-start(f32[128,64]{0,1:T(8,128)} %get-tuple-element.6) | copy-start | bytes 98308
  568.2 10.7 %copy-start.21 = (s32[128,64]{0,1:T(8,128)S(1)}, s32[128,64]{0,1:T(8,128)}, u32[]{:S(2)}) copy-start(s32[128,64]{0,1:T(8,128)} %copy-done.20) | copy-start | bytes 98308
  568.2 10.7 %copy-start.25 = (pred[1024]{0:T(1024)(128)(4,1)S(1)}, pred[1024]{0:T(1024)(128)(4,1)}, u32[]{:S(2)}) copy-start(pred[1024]{0:T(1024)(128)(4,1)} %get-tuple-element.64) | copy-start | bytes 3076
  568.2 10.7 %copy-start.27 = (pred[1024]{0:T(1024)(128)(4,1)S(1)}, pred[1024]{0:T(1024)(128)(4,1)}, u32[]{:S(2)}) copy-start(pred[1024]{0:T(1024)(128)(4,1)} %get-tuple-element.65) | copy-start | bytes 3076
  568.2 10.7 %copy-start.29 = (pred[1024]{0:T(1024)(128)(4,1)S(1)}, pred[1024]{0:T(1024)(128)(4,1)}, u32[]{:S(2)}) copy-start(pred[1024]{0:T(1024)(128)(4,1)} %get-tuple-element.66) | copy-start | bytes 3076
  568.2 10.7 %copy-start.31 = (pred[1024]{0:T(1024)(128)(4,1)S(1)}, pred[1024]{0:T(1024)(128)(4,1)}, u32[]{:S(2)}) copy-start(pred[1024]{0:T(1024)(128)(4,1)} %get-tuple-element.67) | copy-start | bytes 3076
  568.2 10.7 %copy-start.33 = (pred[1024]{0:T(1024)(128)(4,1)S(1)}, pred[1024]{0:T(1024)(128)(4,1)}, u32[]{:S(2)}) copy-start(pred[1024]{0:T(1024)(128)(4,1)} %get-tuple-element.68) | copy-start | bytes 3076
  568.2 10.7 %copy-start.35 = (pred[1024]{0:T(1024)(128)(4,1)S(1)}, pred[1024]{0:T(1024)(128)(4,1)}, u32[]{:S(2)}) copy-start(pred[1024]{0:T(1024)(128)(4,1)} %get-tuple-element.69) | copy-start | bytes 3076
  568.2 10.7 %copy-start.37 = (pred[1024]{0:T(1024)(128)(4,1)S(1)}, pred[1024]{0:T(1024)(128)(4,1)}, u32[]{:S(2)}) copy-start(pred[1024]{0:T(1024)(128)(4,1)} %get-tuple-element.70) | copy-start | bytes 3076
  568.2 67.3 %all-to-all-start.2 = ((bf16[64,16,1152]{2,1,0:T(8,128)(2,1)}), bf16[64,16,1152]{2,1,0:T(8,128)(2,1)S(1)}, u32[]{:S(2)}, u32[]{:S(2)}) async-start(bf16[64,16,1152]{2,1,0:T(8,128)(2,1)} %pad_maximum_fusion.3), calls=%async_computation.4 | async-start | bytes 4718592 | tf_op jit(solution)/shard_map/all_to_all | solution.py:90
  635.5 7.1 %copy-start.2 = (bf16[64,16,1152]{2,1,0:T(8,128)(2,1)}, bf16[64,16,1152]{2,1,0:T(8,128)(2,1)S(1)}, u32[]{:S(2)}) copy-start(bf16[64,16,1152]{2,1,0:T(8,128)(2,1)S(1)} %all-to-all-done.2) | copy-start | bytes 7077892
  635.5 3.0 copy-start.17
  635.5 3.3 copy-start.16
  635.5 3.6 copy-start.15
  637.0 2.4 copy-start.14
  637.0 2.7 copy-start.13
  637.1 3.0 copy-start.12
  638.6 1.8 copy-start.11
  638.6 2.0 copy-start.10
  638.6 2.3 copy-start.9
  638.9 2.3 copy-start.8
  639.2 2.3 copy-start.7
  639.5 2.3 copy-start.6
  640.6 2.3 copy-start.5
  642.9 3.0 copy-start.1
Sparse Core Ops, SparseCore 0:
  211.9 21.1 reduce-scatter.2
  322.2 89.3 all-gather.1
  471.3 92.5 reduce-scatter.4
